TPU v7x, 256 devices: a whole 4x4x8 slice. The times are simulated.
256 devices in a mesh: replica: 4 (over y_lo, core), fsdp: 8 (over z), tensor: 8 (over x, y_hi).
Axes of the slice: x: 4, y: 4 (y_hi: 2, y_lo: 2; y = y_hi * 2 + y_lo), z: 8, core: 2. Of those that a mesh axis runs over, the one named last changes fastest.
Arguments:
- tokens: bfloat16 [16384, 8192], P(('replica', 'fsdp')), may hold values from -6 to 6
- norm_gain: float32 [8192], replicated, may hold values from 0.1 to 1.9
- outer_base: float32 [2, 8192, 1024], P(None, 'fsdp', 'tensor'), may hold values from -0.0625 to 0.0625
- momentum: float32 [2, 8192, 1024], P(None, 'fsdp', 'tensor'), may hold values from -0.06 to 0.06
- inner_params: bfloat16 [4, 2, 8192, 1024], P('replica', None, 'fsdp', 'tensor'), may hold values from -0.0625 to 0.0625
Outputs:
- new_base: float32 [2, 8192, 1024], P(None, ('fsdp', 'replica'), 'tensor')
- new_momentum: float32 [2, 8192, 1024], P(None, ('fsdp', 'replica'), 'tensor')
- keys: bfloat16 [16384, 1024], P(('replica', 'fsdp'), 'tensor')
- values: bfloat16 [16384, 1024], P(('replica', 'fsdp'), 'tensor')
All inputs are finite; a program needn't handle non-finite values.
Results may differ from a plain program's by a relative error of at most 0.018.
Values may be sent and summed in bfloat16 or wider, within the bound.
No kernel may reach another device: no remote copies, remote signals or barrier semaphores. Data moves between devices by JAX's collectives and lax.ppermute only.
A program may use at most 64 MiB of HBM per device.

v0:
```python
import jax
import jax.numpy as jnp
from jax import lax
from jax.sharding import PartitionSpec as P

momentum_rate = 0.9
outer_rate = 0.7
epsilon = 1e-05


def sent_to_all(x, axis):
    copies = jnp.broadcast_to(x, (lax.axis_size(axis), *x.shape))
    return lax.all_to_all(copies, axis, split_axis=0, concat_axis=0, tiled=True)


def taken_together(x, axis):
    everything = sent_to_all(x, axis)
    return jnp.sum(everything.astype(jnp.float32), axis=0)


def normalize(tokens, norm_gain):
    inputs = tokens.astype(jnp.float32)
    scale = lax.rsqrt(jnp.mean(inputs * inputs, axis=-1, keepdims=True) + epsilon)
    return (inputs * scale * norm_gain).astype(jnp.bfloat16)


def nesterov(outer_base, momentum, average):
    new_momentum = momentum_rate * momentum + average
    new_base = outer_base - outer_rate * (average + momentum_rate * new_momentum)
    return (new_base, new_momentum)


def make_adder(normed, portion):
    first = jnp.dot(normed, portion[0], preferred_element_type=jnp.float32)
    second = jnp.dot(normed, portion[1], preferred_element_type=jnp.float32)
    return (first, second)


def on_device(tokens, norm_gain, outer_base, momentum, inner_params):
    normed = normalize(tokens, norm_gain)
    deltas = (outer_base - inner_params[0].astype(jnp.float32)).astype(jnp.bfloat16)
    replicas = lax.axis_size("replica")
    shard_rows = outer_base.shape[1]
    quarter = shard_rows // replicas
    replica_index = lax.axis_index("replica")
    terms = deltas.astype(jnp.float32)
    summed = taken_together(terms.astype(jnp.bfloat16), "replica").astype(jnp.float32)
    full_base, full_momentum = nesterov(outer_base, momentum, summed / replicas)
    weights = full_base.astype(jnp.bfloat16)
    keys, values = make_adder(normed, lax.all_gather(weights, "fsdp", axis=1, tiled=True))
    new_base = lax.dynamic_slice_in_dim(full_base, replica_index * quarter, quarter, 1)
    new_momentum = lax.dynamic_slice_in_dim(full_momentum, replica_index * quarter, quarter, 1)
    return (new_base, new_momentum, keys.astype(jnp.bfloat16), values.astype(jnp.bfloat16))


def solution(mesh):
    placed = (
        P(("replica", "fsdp"), None),
        P(),
        P(None, "fsdp", "tensor"),
        P(None, "fsdp", "tensor"),
        P("replica", None, "fsdp", "tensor"),
    )
    return jax.shard_map(
        on_device,
        mesh=mesh,
        in_specs=placed,
        out_specs=(
            P(None, ("fsdp", "replica"), "tensor"),
            P(None, ("fsdp", "replica"), "tensor"),
            P(("replica", "fsdp"), "tensor"),
            P(("replica", "fsdp"), "tensor"),
        ),
        check_vma=False,
    )
```

profile of v0, /device:TPU:1, one launch (start us, length us, event | category | flops | bytes accessed | tf_op | source)
XLA Modules:
  0.0 117.8 jit_solution(4848803696072113778)
XLA Ops:
  7.2 0.0 copy-start
  7.2 0.0 all-gather.2.cloned.1.call-start
  7.2 0.0 copy-start.1
  7.2 1.6 %fusion.13 = bf16[2,1024,128]{2,1,0:T(8,128)(2,1)S(1)} fusion(f32[2,1024,128]{2,1,0:T(8,128)} %param.7, bf16[1,2,1024,128]{3,2,1,0:T(8,128)(2,1)} %param.9), kind=kLoop, calls=%fused_computation.13 | loop fusion | flops 786432 | bytes 2097152 | tf_op jit(solution)/shard_map/convert_element_type | solution.py:41
  8.8 0.3 broadcast_in_dim.2
  9.1 30.3 %all_to_all.5 = bf16[4,2,1024,128]{3,2,1,0:T(8,128)(2,1)S(1)} all-to-all(bf16[4,2,1024,128]{3,2,1,0:T(8,128)(2,1)S(1)} %broadcast_in_dim.2), channel_id=1, replica_groups=mesh['replica'=4,'fsdp'=8,'tensor'=8] {'replica'}, dimensions={0} | all-to-all | bytes 4194304 | tf_op jit(solution)/shard_map/all_to_all | solution.py:13
  39.4 0.3 convert_reduce_fusion
  39.7 0.0 copy-done
  39.7 0.0 copy-done.1
  39.8 0.0 copy-start.3
  39.8 1.2 fusion.14
  40.9 0.0 all-gather.2.cloned.1.call-update
  41.0 5.1 %fusion = f32[512]{0:T(512)S(1)} fusion(bf16[512,8192]{1,0:T(8,128)(2,1)} %param.5), kind=kLoop, calls=%fused_computation.2 | loop fusion | flops 12582400 | bytes 8390656 | tf_op jit(solution)/shard_map/reduce_sum | solution.py:23
  46.1 0.8 constant_dynamic-slice_fusion
  46.9 50.4 %all-gather.2.cloned.1.call-done = bf16[2,8192,128]{2,1,0:T(8,128)(2,1)} async-done(((bf16[2,1024,128]{2,1,0:T(8,128)(2,1)}), bf16[2,8192,128]{2,1,0:T(8,128)(2,1)}) %all-gather.2.cloned.1.call-update) | async-done | bytes 4194320 | tf_op jit(solution)/shard_map/all_gather | solution.py:50
  97.3 0.0 copy-done.3
  97.3 0.0 copy-start.2
  97.3 7.2 %fusion.10 = bf16[512,128]{1,0:T(8,128)(2,1)} fusion(bf16[2,8192,128]{2,1,0:T(8,128)(2,1)} %all-gather.2.cloned.1.call-done, bf16[512,8192]{1,0:T(8,128)(2,1)} %param.5, f32[8192]{0:T(1024)S(1)} %copy-done.3, f32[512]{0:T(512)S(1)} %add_rsqrt_fusion), kind=kOutput, calls=%fused_computation.11 | convolution fusion | flops 1090584576 | bytes 10651648 | tf_op jit(solution)/shard_map/dot_general | solution.py:35
  104.5 0.0 copy-done.2
  104.5 6.4 %fusion.7 = bf16[512,128]{1,0:T(8,128)(2,1)} fusion(bf16[2,8192,128]{2,1,0:T(8,128)(2,1)S(1)} %copy-done.2, bf16[512,8192]{1,0:T(8,128)(2,1)} %param.5, f32[8192]{0:T(1024)S(1)} %copy-done.3, f32[512]{0:T(512)S(1)} %add_rsqrt_fusion), kind=kOutput, calls=%fused_computation.10 | convolution fusion | flops 1090584576 | bytes 10651648 | tf_op jit(solution)/shard_map/dot_general | solution.py:34
  (1 shorter events, 0.0 us)
Async XLA Ops:
  7.2 32.6 %copy-start = (f32[2,1024,128]{2,1,0:T(8,128)S(1)}, f32[2,1024,128]{2,1,0:T(8,128)}, u32[]{:S(2)}) copy-start(f32[2,1024,128]{2,1,0:T(8,128)} %param.7) | copy-start | bytes 3145732
  7.2 90.2 %all-gather.2.cloned.1.call-start = ((), (), s32[]{:S(2)}) async-start(), calls=%async_computation.1 | async-start | bytes 4718592 | tf_op jit(solution)/shard_map/all_gather | solution.py:50
  7.2 32.5 %copy-start.1 = (f32[2,1024,128]{2,1,0:T(8,128)S(1)}, f32[2,1024,128]{2,1,0:T(8,128)}, u32[]{:S(2)}) copy-start(f32[2,1024,128]{2,1,0:T(8,128)} %param.8) | copy-start | bytes 3145732
  39.8 57.6 %copy-start.3 = (f32[8192]{0:T(1024)S(1)}, f32[8192]{0:T(1024)}, u32[]{:S(2)}) copy-start(f32[8192]{0:T(1024)} %param.6) | copy-start | bytes 98308
  97.3 7.2 %copy-start.2 = (bf16[2,8192,128]{2,1,0:T(8,128)(2,1)S(1)}, bf16[2,8192,128]{2,1,0:T(8,128)(2,1)}, u32[]{:S(2)}) copy-start(bf16[2,8192,128]{2,1,0:T(8,128)(2,1)} %all-gather.2.cloned.1.call-done) | copy-start | bytes 12582916
Sparse Core Ops, SparseCore 0:
  41.1 56.2 all-gather.1
where the time goes:
time: 118 us
  waiting for transfers between devices  50.4 us (43%)
  blocking collectives  30.3 us (26%)
  between operations  14.1 us (12%)
  matrix products  13.6 us (12%)
  other arithmetic  8.2 us (7%)
    all_gather x1, waiting for transfers between devices, on_device(): lax.all_gather(weights, 'fsdp', axis=1, tiled=True)  50.4 us
    all_to_all x1, blocking collectives, sent_to_all(): return lax.all_to_all(copies, axis, split_axis=0, concat_axis=0, tiled=True)  30.3 us
    dot_general x1, matrix products, make_adder(): second = jnp.dot(normed, portion[1], preferred_element_type=jnp.float32)  7.16 us
    dot_general x1, matrix products, make_adder(): first = jnp.dot(normed, portion[0], preferred_element_type=jnp.float32)  6.43 us
    reduce_sum x1, other arithmetic, normalize(): jnp.mean(inputs * inputs, axis=-1, keepdims=True) + epsilon  5.1 us
  transfers between devices with their start and end apart: 1, of which 1 were waited for; matrix products, arithmetic and copies ran while one was open for 5% of the time, Pallas kernels for 0%

commit v1 on v0

--- a/solution.py
+++ b/solution.py
@@ -6,6 +6,22 @@
 momentum_rate = 0.9
 outer_rate = 0.7
 epsilon = 1e-05
+
+
+def collect(x, axis, dim):
+    ways, here, turn = (lax.axis_size(axis), lax.axis_index(axis), x.shape[dim])
+    dims = [n * ways if d == dim else n for d, n in enumerate(x.shape)]
+    full = lax.dynamic_update_slice_in_dim(jnp.zeros(dims, x.dtype), x, here * turn, axis=dim)
+    going_up = going_down = x
+    for far in range(1, ways // 2 + 1):
+        going_up = lax.ppermute(going_up, axis, [(d, (d + 1) % ways) for d in range(ways)])
+        full = lax.dynamic_update_slice_in_dim(full, going_up, (here - far) % ways * turn, axis=dim)
+        if 2 * far < ways:
+            going_down = lax.ppermute(going_down, axis, [(d, (d - 1) % ways) for d in range(ways)])
+            full = lax.dynamic_update_slice_in_dim(
+                full, going_down, (here + far) % ways * turn, axis=dim
+            )
+    return full
 
 
 def sent_to_all(x, axis):
@@ -47,7 +63,7 @@
     summed = taken_together(terms.astype(jnp.bfloat16), "replica").astype(jnp.float32)
     full_base, full_momentum = nesterov(outer_base, momentum, summed / replicas)
     weights = full_base.astype(jnp.bfloat16)
-    keys, values = make_adder(normed, lax.all_gather(weights, "fsdp", axis=1, tiled=True))
+    keys, values = make_adder(normed, collect(weights, "fsdp", 1))
     new_base = lax.dynamic_slice_in_dim(full_base, replica_index * quarter, quarter, 1)
     new_momentum = lax.dynamic_slice_in_dim(full_momentum, replica_index * quarter, quarter, 1)
     return (new_base, new_momentum, keys.astype(jnp.bfloat16), values.astype(jnp.bfloat16))

time: 118 us -> 110 us (0.932)
  the two profiles are of different devices: /device:TPU:1 before, /device:TPU:30 now
where the time goes in v1:
time: 110 us
  waiting for transfers between devices  54.7 us (50%)
  starting transfers between devices  17.2 us (16%)
  local copies, waits for them, and re-layouts  15.2 us (14%)
  matrix products  12.3 us (11%)
  other arithmetic  9.69 us (9%)
    ppermute x4, waiting for transfers between devices, collect(): lax.ppermute(going_up, axis, [(d, (d + 1) % ways) for d in range(ways)])  27.2 us
    all_to_all x1, waiting for transfers between devices, sent_to_all(): return lax.all_to_all(copies, axis, split_axis=0, concat_axis=0, tiled=True)  24 us
    ppermute x3, starting transfers between devices, collect(): lax.ppermute(going_down, axis, [(d, (d - 1) % ways) for d in range(ways)])  10.9 us
    dot_general x1, matrix products, make_adder(): first = jnp.dot(normed, portion[0], preferred_element_type=jnp.float32)  7.63 us
    dynamic_update_slice x4, local copies, waits for them, and re-layouts, collect(): lax.dynamic_update_slice_in_dim(full, going_up, (here - far) % ways * tur...  5.56 us
    reduce_sum x1, other arithmetic, normalize(): jnp.mean(inputs * inputs, axis=-1, keepdims=True) + epsilon  5.1 us
    dot_general x1, matrix products, make_adder(): second = jnp.dot(normed, portion[1], preferred_element_type=jnp.float32)  4.7 us
    dynamic_update_slice x3, local copies, waits for them, and re-layouts, collect(): lax.dynamic_update_slice_in_dim(full, going_down, (here + far) % ways * t...  4.7 us
  transfers between devices with their start and end apart: 8, of which 6 were waited for; matrix products, arithmetic and copies ran while one was open for 14% of the time, Pallas kernels for 0%

profile of v1, /device:TPU:30, one launch (start us, length us, event | category | flops | bytes accessed | tf_op | source)
XLA Modules:
  0.0 109.7 jit_solution(16879881470402085400)
XLA Ops:
  0.6 1.5 %fusion.13 = bf16[2,1024,128]{2,1,0:T(8,128)(2,1)S(1)} fusion(f32[2,1024,128]{2,1,0:T(8,128)} %param.7, bf16[1,2,1024,128]{3,2,1,0:T(8,128)(2,1)} %param.9), kind=kLoop, calls=%fused_computation.13 | loop fusion | flops 786432 | bytes 2097152 | tf_op jit(solution)/shard_map/convert_element_type | solution.py:57
  2.1 1.6 %broadcast_in_dim.8 = bf16[4,2,1024,128]{3,2,1,0:T(8,128)(2,1)} broadcast(bf16[2,1024,128]{2,1,0:T(8,128)(2,1)S(1)} %fusion.13), dimensions={1,2,3} | broadcast | bytes 2621440 | tf_op jit(solution)/shard_map/broadcast_in_dim | solution.py:28
  3.7 4.3 %all-to-all-start = ((bf16[4,2,1024,128]{3,2,1,0:T(8,128)(2,1)}), bf16[4,2,1024,128]{3,2,1,0:T(8,128)(2,1)S(1)}, u32[]{:S(2)}, u32[]{:S(2)}) async-start(bf16[4,2,1024,128]{3,2,1,0:T(8,128)(2,1)} %broadcast_in_dim.8), calls=%async_computation | async-start | bytes 4194304 | tf_op jit(solution)/shard_map/all_to_all | solution.py:29
  8.0 24.0 %all-to-all-done = bf16[4,2,1024,128]{3,2,1,0:T(8,128)(2,1)S(1)} async-done(((bf16[4,2,1024,128]{3,2,1,0:T(8,128)(2,1)}), bf16[4,2,1024,128]{3,2,1,0:T(8,128)(2,1)S(1)}, u32[]{:S(2)}, u32[]{:S(2)}) %all-to-all-start) | async-done | bytes 2097184 | tf_op jit(solution)/shard_map/all_to_all | solution.py:29
  32.1 0.3 convert_reduce_fusion
  32.4 2.5 %broadcast_in_dim.9 = bf16[2,8192,128]{2,1,0:T(8,128)(2,1)} broadcast(bf16[]{:T(256)} %constant.73.clone.1), dimensions={} | broadcast | bytes 4194306 | tf_op jit(solution)/shard_map/broadcast_in_dim | solution.py:14
  34.9 2.7 %constant_dynamic-update-slice_fusion.7 = (bf16[2,8192,128]{2,1,0:T(8,128)(2,1)}, bf16[2,1024,128]{2,1,0:T(8,128)(2,1)S(1)}, f32[2,1024,128]{2,1,0:T(8,128)S(1)}) fusion(bf16[2,8192,128]{2,1,0:T(8,128)(2,1)} %broadcast_in_dim.9, s32[]{:T(128)S(6)} %select_n.60, f32[2,1024,128]{2,1,0:T(8,128)} %param.7, f32[2,1024,128]{2,1,0:T(8,128)} %param.8, ...), kind=kLoop, calls=%fused_computation.23 | loop fusion | flops 2097152 | bytes 5242884 | tf_op jit(solution)/shard_map/dynamic_update_slice | solution.py:14
  37.5 0.0 copy-start
  37.5 1.9 %collective-permute-start = (bf16[2,1024,128]{2,1,0:T(8,128)(2,1)S(1)}, bf16[2,1024,128]{2,1,0:T(8,128)(2,1)}, u32[]{:S(2)}, u32[]{:S(2)}) collective-permute-start(bf16[2,1024,128]{2,1,0:T(8,128)(2,1)S(1)} %get-tuple-element.5), channel_id=1, source_target_pairs={{0,8},{8,16},{16,24},{24,32},{32,40},{40,48},{48,56},{56,0},{1,9},... | collective-permute-start | bytes 1572872 | tf_op jit(solution)/shard_map/ppermute | solution.py:17
  39.5 3.9 %collective-permute-start.1 = (bf16[2,1024,128]{2,1,0:T(8,128)(2,1)S(1)}, bf16[2,1024,128]{2,1,0:T(8,128)(2,1)}, u32[]{:S(2)}, u32[]{:S(2)}) collective-permute-start(bf16[2,1024,128]{2,1,0:T(8,128)(2,1)S(1)} %get-tuple-element.5), channel_id=1, source_target_pairs={{0,56},{8,0},{16,8},{24,16},{32,24},{40,32},{48,40},{56,48},{1,57}... | collective-permute-start | bytes 1572872 | tf_op jit(solution)/shard_map/ppermute | solution.py:20
  43.4 12.1 %collective-permute-done = bf16[2,1024,128]{2,1,0:T(8,128)(2,1)} collective-permute-done((bf16[2,1024,128]{2,1,0:T(8,128)(2,1)S(1)}, bf16[2,1024,128]{2,1,0:T(8,128)(2,1)}, u32[]{:S(2)}, u32[]{:S(2)}) %collective-permute-start) | collective-permute-done | bytes 524320 | tf_op jit(solution)/shard_map/ppermute | solution.py:17
  55.5 0.0 collective-permute-start.2
  55.5 5.1 %fusion = f32[512]{0:T(512)S(1)} fusion(bf16[512,8192]{1,0:T(8,128)(2,1)} %param.5), kind=kLoop, calls=%fused_computation.2 | loop fusion | flops 12582400 | bytes 8390656 | tf_op jit(solution)/shard_map/reduce_sum | solution.py:39
  60.6 0.0 collective-permute-done.1
  60.6 3.3 %collective-permute-start.3 = (bf16[2,1024,128]{2,1,0:T(8,128)(2,1)}, bf16[2,1024,128]{2,1,0:T(8,128)(2,1)}, u32[]{:S(2)}, u32[]{:S(2)}) collective-permute-start(bf16[2,1024,128]{2,1,0:T(8,128)(2,1)} %collective-permute-done.1), channel_id=1, source_target_pairs={{0,56},{8,0},{16,8},{24,16},{32,24},{40,32},{48,40},{56,48},{1,57}... | collective-permute-start | bytes 1572872 | tf_op jit(solution)/shard_map/ppermute | solution.py:20
  63.9 6.3 %collective-permute-done.2 = bf16[2,1024,128]{2,1,0:T(8,128)(2,1)} collective-permute-done((bf16[2,1024,128]{2,1,0:T(8,128)(2,1)}, bf16[2,1024,128]{2,1,0:T(8,128)(2,1)}, u32[]{:S(2)}, u32[]{:S(2)}) %collective-permute-start.2) | collective-permute-done | bytes 524320 | tf_op jit(solution)/shard_map/ppermute | solution.py:17
  70.2 0.0 collective-permute-start.4
  70.2 0.0 copy-done
  70.2 0.1 multiply_add_fusion
  70.3 0.0 copy-start.1
  70.3 0.8 constant_dynamic-slice_fusion
  71.2 3.5 %collective-permute-done.3 = bf16[2,1024,128]{2,1,0:T(8,128)(2,1)} collective-permute-done((bf16[2,1024,128]{2,1,0:T(8,128)(2,1)}, bf16[2,1024,128]{2,1,0:T(8,128)(2,1)}, u32[]{:S(2)}, u32[]{:S(2)}) %collective-permute-start.3) | collective-permute-done | bytes 524320 | tf_op jit(solution)/shard_map/ppermute | solution.py:20
  74.6 3.7 %collective-permute-start.5 = (bf16[2,1024,128]{2,1,0:T(8,128)(2,1)}, bf16[2,1024,128]{2,1,0:T(8,128)(2,1)S(1)}, u32[]{:S(2)}, u32[]{:S(2)}) collective-permute-start(bf16[2,1024,128]{2,1,0:T(8,128)(2,1)} %collective-permute-done.3), channel_id=1, source_target_pairs={{0,56},{8,0},{16,8},{24,16},{32,24},{40,32},{48,40},{56,48},{1,57}... | collective-permute-start | bytes 1572872 | tf_op jit(solution)/shard_map/ppermute | solution.py:20
  78.3 1.9 %constant_dynamic-update-slice_fusion.6 = bf16[2,8192,128]{2,1,0:T(8,128)(2,1)} fusion(bf16[2,8192,128]{2,1,0:T(8,128)(2,1)} %get-tuple-element.4, bf16[2,1024,128]{2,1,0:T(8,128)(2,1)} %collective-permute-done, s32[]{:T(128)S(6)} %select_n.62), kind=kLoop, calls=%fused_computation.22 | loop fusion | bytes 1048580 | tf_op jit(solution)/shard_map/dynamic_update_slice | solution.py:18
  80.2 3.7 %collective-permute-done.4 = bf16[2,1024,128]{2,1,0:T(8,128)(2,1)S(1)} collective-permute-done((bf16[2,1024,128]{2,1,0:T(8,128)(2,1)}, bf16[2,1024,128]{2,1,0:T(8,128)(2,1)S(1)}, u32[]{:S(2)}, u32[]{:S(2)}) %collective-permute-start.4) | collective-permute-done | bytes 524320 | tf_op jit(solution)/shard_map/ppermute | solution.py:17
  83.9 0.0 collective-permute-start.6
  83.9 1.9 %constant_dynamic-update-slice_fusion.5 = bf16[2,8192,128]{2,1,0:T(8,128)(2,1)} fusion(bf16[2,8192,128]{2,1,0:T(8,128)(2,1)} %constant_dynamic-update-slice_fusion.6, bf16[2,1024,128]{2,1,0:T(8,128)(2,1)} %collective-permute-done.1, s32[]{:T(128)S(6)} %select_n.64), kind=kLoop, calls=%fused_computation.21 | loop fusion | bytes 1048580 | tf_op jit(solution)/shard_map/dynamic_update_slice | solution.py:21
  85.8 1.9 %constant_dynamic-update-slice_fusion.4 = bf16[2,8192,128]{2,1,0:T(8,128)(2,1)} fusion(bf16[2,8192,128]{2,1,0:T(8,128)(2,1)} %constant_dynamic-update-slice_fusion.5, bf16[2,1024,128]{2,1,0:T(8,128)(2,1)} %collective-permute-done.2, s32[]{:T(128)S(6)} %select_n.66), kind=kLoop, calls=%fused_computation.20 | loop fusion | bytes 1048580 | tf_op jit(solution)/shard_map/dynamic_update_slice | solution.py:18
  87.8 1.9 %constant_dynamic-update-slice_fusion.3 = bf16[2,8192,128]{2,1,0:T(8,128)(2,1)} fusion(bf16[2,8192,128]{2,1,0:T(8,128)(2,1)} %constant_dynamic-update-slice_fusion.4, bf16[2,1024,128]{2,1,0:T(8,128)(2,1)} %collective-permute-done.3, s32[]{:T(128)S(6)} %select_n.68), kind=kLoop, calls=%fused_computation.19 | loop fusion | bytes 1048580 | tf_op jit(solution)/shard_map/dynamic_update_slice | solution.py:21
  89.7 0.9 constant_dynamic-update-slice_fusion.2
  90.6 0.0 collective-permute-done.5
  90.6 0.8 constant_dynamic-update-slice_fusion.1
  91.4 5.1 %collective-permute-done.6 = bf16[2,1024,128]{2,1,0:T(8,128)(2,1)S(1)} collective-permute-done((bf16[2,1024,128]{2,1,0:T(8,128)(2,1)S(1)}, bf16[2,1024,128]{2,1,0:T(8,128)(2,1)S(1)}, u32[]{:S(2)}, u32[]{:S(2)}) %collective-permute-start.6) | collective-permute-done | bytes 524320 | tf_op jit(solution)/shard_map/ppermute | solution.py:17
  96.6 0.0 slice-start
  96.6 0.8 constant_dynamic-update-slice_fusion
  97.4 0.0 copy-done.1
  97.4 0.0 slice-start.1
  97.4 7.6 %fusion.7 = bf16[512,128]{1,0:T(8,128)(2,1)} fusion(bf16[2,8192,128]{2,1,0:T(8,128)(2,1)} %constant_dynamic-update-slice_fusion, bf16[512,8192]{1,0:T(8,128)(2,1)} %param.5, f32[8192]{0:T(1024)S(1)} %copy-done.1, f32[512]{0:T(512)S(1)} %add_rsqrt_fusion), kind=kOutput, calls=%fused_computation.10 | convolution fusion | flops 1090584576 | bytes 10651648 | tf_op jit(solution)/shard_map/dot_general | solution.py:50
  105.0 0.0 slice-done
  105.0 0.0 slice-done.1
  105.0 4.7 %fusion.10 = bf16[512,128]{1,0:T(8,128)(2,1)} fusion(bf16[2,8192,128]{2,1,0:T(8,128)(2,1)} %constant_dynamic-update-slice_fusion, bf16[512,8192]{1,0:T(8,128)(2,1)S(1)} %bitcast.14, f32[8192]{0:T(1024)S(1)} %copy-done.1, f32[512]{0:T(512)S(1)} %add_rsqrt_fusion), kind=kOutput, calls=%fused_computation.11 | convolution fusion | flops 1090584576 | bytes 10651648 | tf_op jit(solution)/shard_map/dot_general | solution.py:51
  (2 shorter events, 0.0 us)
Async XLA Ops:
  3.7 28.4 %all-to-all-start = ((bf16[4,2,1024,128]{3,2,1,0:T(8,128)(2,1)}), bf16[4,2,1024,128]{3,2,1,0:T(8,128)(2,1)S(1)}, u32[]{:S(2)}, u32[]{:S(2)}) async-start(bf16[4,2,1024,128]{3,2,1,0:T(8,128)(2,1)} %broadcast_in_dim.8), calls=%async_computation | async-start | bytes 4194304 | tf_op jit(solution)/shard_map/all_to_all | solution.py:29
  37.5 32.6 %copy-start = (f32[2,1024,128]{2,1,0:T(8,128)S(1)}, f32[2,1024,128]{2,1,0:T(8,128)}, u32[]{:S(2)}) copy-start(f32[2,1024,128]{2,1,0:T(8,128)} %param.8) | copy-start | bytes 3145732
  37.5 17.9 %collective-permute-start = (bf16[2,1024,128]{2,1,0:T(8,128)(2,1)S(1)}, bf16[2,1024,128]{2,1,0:T(8,128)(2,1)}, u32[]{:S(2)}, u32[]{:S(2)}) collective-permute-start(bf16[2,1024,128]{2,1,0:T(8,128)(2,1)S(1)} %get-tuple-element.5), channel_id=1, source_target_pairs={{0,8},{8,16},{16,24},{24,32},{32,40},{40,48},{48,56},{56,0},{1,9},... | collective-permute-start | bytes 1572872 | tf_op jit(solution)/shard_map/ppermute | solution.py:17
  39.5 21.1 %collective-permute-start.1 = (bf16[2,1024,128]{2,1,0:T(8,128)(2,1)S(1)}, bf16[2,1024,128]{2,1,0:T(8,128)(2,1)}, u32[]{:S(2)}, u32[]{:S(2)}) collective-permute-start(bf16[2,1024,128]{2,1,0:T(8,128)(2,1)S(1)} %get-tuple-element.5), channel_id=1, source_target_pairs={{0,56},{8,0},{16,8},{24,16},{32,24},{40,32},{48,40},{56,48},{1,57}... | collective-permute-start | bytes 1572872 | tf_op jit(solution)/shard_map/ppermute | solution.py:20
  55.5 14.7 %collective-permute-start.2 = (bf16[2,1024,128]{2,1,0:T(8,128)(2,1)}, bf16[2,1024,128]{2,1,0:T(8,128)(2,1)}, u32[]{:S(2)}, u32[]{:S(2)}) collective-permute-start(bf16[2,1024,128]{2,1,0:T(8,128)(2,1)} %collective-permute-done), channel_id=1, source_target_pairs={{0,8},{8,16},{16,24},{24,32},{32,40},{40,48},{48,56},{56,0},{1,9},... | collective-permute-start | bytes 1572872 | tf_op jit(solution)/shard_map/ppermute | solution.py:17
  60.6 14.0 %collective-permute-start.3 = (bf16[2,1024,128]{2,1,0:T(8,128)(2,1)}, bf16[2,1024,128]{2,1,0:T(8,128)(2,1)}, u32[]{:S(2)}, u32[]{:S(2)}) collective-permute-start(bf16[2,1024,128]{2,1,0:T(8,128)(2,1)} %collective-permute-done.1), channel_id=1, source_target_pairs={{0,56},{8,0},{16,8},{24,16},{32,24},{40,32},{48,40},{56,48},{1,57}... | collective-permute-start | bytes 1572872 | tf_op jit(solution)/shard_map/ppermute | solution.py:20
  70.2 13.7 %collective-permute-start.4 = (bf16[2,1024,128]{2,1,0:T(8,128)(2,1)}, bf16[2,1024,128]{2,1,0:T(8,128)(2,1)S(1)}, u32[]{:S(2)}, u32[]{:S(2)}) collective-permute-start(bf16[2,1024,128]{2,1,0:T(8,128)(2,1)} %collective-permute-done.2), channel_id=1, source_target_pairs={{0,8},{8,16},{16,24},{24,32},{32,40},{40,48},{48,56},{56,0},{1,9},... | collective-permute-start | bytes 1572872 | tf_op jit(solution)/shard_map/ppermute | solution.py:17
  70.3 27.1 %copy-start.1 = (f32[8192]{0:T(1024)S(1)}, f32[8192]{0:T(1024)}, u32[]{:S(2)}) copy-start(f32[8192]{0:T(1024)} %param.6) | copy-start | bytes 98308
  74.6 15.9 %collective-permute-start.5 = (bf16[2,1024,128]{2,1,0:T(8,128)(2,1)}, bf16[2,1024,128]{2,1,0:T(8,128)(2,1)S(1)}, u32[]{:S(2)}, u32[]{:S(2)}) collective-permute-start(bf16[2,1024,128]{2,1,0:T(8,128)(2,1)} %collective-permute-done.3), channel_id=1, source_target_pairs={{0,56},{8,0},{16,8},{24,16},{32,24},{40,32},{48,40},{56,48},{1,57}... | collective-permute-start | bytes 1572872 | tf_op jit(solution)/shard_map/ppermute | solution.py:20
  83.9 12.7 %collective-permute-start.6 = (bf16[2,1024,128]{2,1,0:T(8,128)(2,1)S(1)}, bf16[2,1024,128]{2,1,0:T(8,128)(2,1)S(1)}, u32[]{:S(2)}, u32[]{:S(2)}) collective-permute-start(bf16[2,1024,128]{2,1,0:T(8,128)(2,1)S(1)} %collective-permute-done.4), channel_id=1, source_target_pairs={{0,8},{8,16},{16,24},{24,32},{32,40},{40,48},{48,56},{56,0},{1,9},... | collective-permute-start | bytes 1572872 | tf_op jit(solution)/shard_map/ppermute | solution.py:17
  96.6 8.5 %slice-start = ((s8[8388608]{0:T(1024)(128)(4,1)}), s8[4194304]{0:T(1024)(128)(4,1)S(1)}, s32[]{:S(2)}) async-start(s8[8388608]{0:T(1024)(128)(4,1)} %bitcast.13), calls=%async_computation.1 | async-start | bytes 8388608
  97.4 7.6 %slice-start.1 = ((s8[8388608]{0:T(1024)(128)(4,1)}), s8[4194304]{0:T(1024)(128)(4,1)S(1)}, s32[]{:S(2)}) async-start(s8[8388608]{0:T(1024)(128)(4,1)} %bitcast.13), calls=%async_computation.2 | async-start | bytes 8388608
